TPU v7x, 32 devices: a whole 2x2x4 slice. The times are simulated.
32 devices in a mesh: dp: 4 (over y, core), tensor: 8 (over z, x).
Axes of the slice: x: 2, y: 2, z: 4, core: 2. Of those that a mesh axis runs over, the one named last changes fastest.
Arguments:
- tokens: bfloat16 [8192, 2048], P(('dp', 'tensor')), may hold values from -6 to 6
- segment_ids: int32 [4, 2048], P('dp'), may hold values from 0 to 3, never falling along the last dimension, each value on 1 to 1024 neighbouring positions
- first_gain: bfloat16 [2048], replicated, may hold values from 0.5 to 1.5
- first_shift: bfloat16 [2048], replicated, may hold values from -3 to 3
- second_gain: bfloat16 [2048], replicated, may hold values from 0.5 to 1.5
- second_shift: bfloat16 [2048], replicated, may hold values from -3 to 3
- qkv_weight: bfloat16 [2048, 8, 768], P('dp', 'tensor'), may hold values from -0.125 to 0.125
- qkv_bias: bfloat16 [8, 768], P('tensor'), may hold values from -3 to 3
- out_weight: bfloat16 [2048, 2048], P('tensor', 'dp'), may hold values from -1 to 1
- out_bias: bfloat16 [2048], replicated, may hold values from -3 to 3
- up_projection_weight: bfloat16 [2048, 8192], P('dp', 'tensor'), may hold values from -0.125 to 0.125
- up_bias: bfloat16 [8192], P('tensor'), may hold values from -3 to 3
- down_weight: bfloat16 [8192, 2048], P('tensor', 'dp'), may hold values from -0.0625 to 0.0625
- down_bias: bfloat16 [2048], replicated, may hold values from -3 to 3
- cotangent: bfloat16 [8192, 2048], P(('dp', 'tensor')), may hold values from -6 to 6
Outputs:
- output: bfloat16 [8192, 2048], P(('dp', 'tensor'))
- layer_input_gradient: float32 [8192, 2048], P(('dp', 'tensor'))
- first_gain_grad: float32 [2048], replicated
- first_shift_grad: float32 [2048], replicated
- second_gain_grad: float32 [2048], replicated
- second_shift_grad: float32 [2048], replicated
- qkv_weight_grad: float32 [2048, 8, 768], P('dp', 'tensor')
- qkv_bias_grad: float32 [8, 768], P('tensor')
- out_weight_grad: float32 [2048, 2048], P('tensor', 'dp')
- out_bias_grad: float32 [2048], replicated
- up_weight_grad: float32 [2048, 8192], P('dp', 'tensor')
- up_bias_grad: float32 [8192], P('tensor')
- down_weight_grad: float32 [8192, 2048], P('tensor', 'dp')
- down_bias_grad: float32 [2048], replicated
Inputs may be any that keep to these rules, and one draw needn't show every extreme that they name: `segment_ids`: within each group the segment numbers never fall; each sequence has 1 to 1024 tokens and one of them exactly 1024; every number up to the largest occurs.
All inputs are finite; a program needn't handle non-finite values.
Results may differ from a plain program's by a relative error of at most 0.014.
Values may be sent and summed in bfloat16 or wider, within the bound.
No kernel may reach another device: no remote copies, remote signals or barrier semaphores. Data moves between devices by JAX's collectives and lax.ppermute only.
A program may use at most 192 MiB of HBM per device.

v0:
```python
from functools import partial
import math

import jax
import jax.numpy as jnp
from jax import lax
from jax.sharding import PartitionSpec as P

HD = 256
ROT = 64


NORM_EPS = 1e-05
MASK_FILL = -1e30


def normalize(values):
    mean_val = jnp.mean(values, axis=-1, keepdims=True)
    centred = values - mean_val
    spread = jnp.mean(centred * centred, axis=-1, keepdims=True)
    inv_std = lax.rsqrt(spread + NORM_EPS)
    return (centred * inv_std, inv_std)


def positions_of(segment):
    row_count = segment.shape[0]
    position_index = jnp.arange(row_count, dtype=jnp.int32)
    starts = jnp.concatenate([jnp.ones((1,), dtype=jnp.bool_), segment[1:] != segment[:-1]])
    first_index = lax.cummax(
        jnp.where(starts, position_index, jnp.zeros_like(position_index)), axis=0
    )
    return position_index - first_index


def rotation_tables(position):
    half_dims = ROT // 2
    inv_freq = 10000.0 ** (-2.0 * jnp.arange(half_dims, dtype=jnp.float32) / ROT)
    angles = position.astype(jnp.float32)[:, None] * inv_freq[None, :]
    return (jnp.cos(angles), jnp.sin(angles))


def rotate(values, cosine_table, sine_table, direction):
    half_dims = ROT // 2
    leading = values[:, :half_dims]
    trailing = values[:, half_dims:ROT]
    return jnp.concatenate(
        [
            leading * cosine_table - direction * trailing * sine_table,
            trailing * cosine_table + direction * leading * sine_table,
            values[:, ROT:],
        ],
        axis=1,
    )


def body(
    tokens,
    segment_ids,
    first_gain,
    first_shift,
    second_gain,
    second_shift,
    qkv_weight,
    qkv_bias,
    out_weight,
    out_bias,
    up_projection_weight,
    up_bias,
    down_weight,
    down_bias,
    cotangent,
):
    width = tokens.shape[1]
    heads_here = qkv_weight.shape[1]
    qkv_cols = heads_here * 3 * HD
    attn_cols = heads_here * HD
    segment = segment_ids[0]
    group_rows = segment.shape[0]
    block_rows = min(512, group_rows)
    block_count = group_rows // block_rows
    position = positions_of(segment)
    cosine_table, sine_table = rotation_tables(position)
    position_index = jnp.arange(group_rows, dtype=jnp.int32)
    score_scale = 1.0 / math.sqrt(HD)
    x_values = tokens.astype(jnp.float32)
    normed, inv_std = normalize(x_values)
    first_gain_f = first_gain.astype(jnp.float32)
    second_gain_f = second_gain.astype(jnp.float32)
    normed_local = normed.astype(jnp.bfloat16)
    normed_all = lax.all_gather(normed_local, "tensor", axis=0, tiled=True).astype(jnp.float32)
    first_all = (normed_all * first_gain_f + first_shift.astype(jnp.float32)).astype(jnp.bfloat16)
    second_all = (normed_all * second_gain_f + second_shift.astype(jnp.float32)).astype(
        jnp.bfloat16
    )
    joined_in = jnp.concatenate(
        [qkv_weight.reshape(qkv_weight.shape[0], qkv_cols), up_projection_weight], axis=1
    )
    joined_out = jnp.concatenate([out_weight, down_weight], axis=0)
    weight_piece = lax.all_gather(joined_in, "dp", axis=0, tiled=True)
    left_cols = first_all
    right_cols = second_all
    proj = jnp.dot(left_cols, weight_piece[:, :qkv_cols], preferred_element_type=jnp.float32)
    up_preactivation = jnp.dot(
        right_cols, weight_piece[:, qkv_cols:], preferred_element_type=jnp.float32
    )
    proj = proj.reshape(group_rows, heads_here, 3 * HD) + qkv_bias.astype(jnp.float32)[None]
    up_preactivation = up_preactivation + up_bias.astype(jnp.float32)[None]
    query_heads, key_heads, value_heads = ([], [], [])
    head_index = 0
    head_proj = proj[:, head_index]
    query_heads.append(
        rotate(head_proj[:, :HD], cosine_table, sine_table, 1.0).astype(jnp.bfloat16)
    )
    key_heads.append(
        rotate(head_proj[:, HD : 2 * HD], cosine_table, sine_table, 1.0).astype(jnp.bfloat16)
    )
    value_heads.append(head_proj[:, 2 * HD :].astype(jnp.bfloat16))

    def block_scores(query_block, key_rows, row_start, key_count):
        raw = (
            jnp.einsum("qd,kd->qk", query_block, key_rows, preferred_element_type=jnp.float32)
            * score_scale
        )
        seg_query = segment[row_start : row_start + block_rows]
        allowed = (seg_query[:, None] == segment[None, :key_count]) & (
            position_index[row_start : row_start + block_rows, None]
            >= position_index[None, :key_count]
        )
        return jnp.where(allowed, raw, MASK_FILL)

    attn_heads, lse_heads = ([], [])
    head_index = 0
    rows_out = []
    lse_rows = []
    for block_index in range(block_count):
        row_start = block_index * block_rows
        key_count = row_start + block_rows
        scores = block_scores(
            query_heads[head_index][row_start:key_count],
            key_heads[head_index][:key_count],
            row_start,
            key_count,
        )
        row_top = jnp.max(scores, axis=1, keepdims=True)
        exp_scores = jnp.exp(scores - row_top)
        row_total = jnp.sum(exp_scores, axis=1, keepdims=True)
        probs_low = (exp_scores / row_total).astype(jnp.bfloat16)
        rows_out.append(
            jnp.dot(
                probs_low, value_heads[head_index][:key_count], preferred_element_type=jnp.float32
            ).astype(jnp.bfloat16)
        )
        lse_rows.append(row_top + jnp.log(row_total))
    attn_heads.append(jnp.concatenate(rows_out, axis=0))
    lse_heads.append(jnp.concatenate(lse_rows, axis=0))
    attn = attn_heads[0]
    act = jax.nn.gelu(up_preactivation, approximate=False).astype(jnp.bfloat16)
    mixed = jnp.concatenate([attn, act], axis=1)
    incomplete_sum = jnp.dot(
        mixed,
        lax.all_gather(joined_out, "dp", axis=1, tiled=True),
        preferred_element_type=jnp.float32,
    )
    summed = lax.psum_scatter(
        incomplete_sum.astype(jnp.bfloat16), "tensor", scatter_dimension=0, tiled=True
    ).astype(jnp.float32)
    output = (
        x_values + out_bias.astype(jnp.float32) + down_bias.astype(jnp.float32) + summed
    ).astype(jnp.bfloat16)
    cot_all = lax.all_gather(cotangent, "tensor", axis=0, tiled=True)
    cot_cols = cot_all
    back_mixed = jnp.einsum(
        "gd,fd->gf",
        cot_cols,
        lax.all_gather(joined_out, "dp", axis=1, tiled=True),
        preferred_element_type=jnp.float32,
    )
    d_attn = back_mixed[:, :attn_cols].astype(jnp.bfloat16)
    gelu_pull = jax.vjp(partial(jax.nn.gelu, approximate=False), up_preactivation)[1]
    d_up = gelu_pull(back_mixed[:, attn_cols:])[0].astype(jnp.bfloat16)
    head_index = 0
    query_grads = []
    key_grad = jnp.zeros((group_rows, HD), jnp.float32)
    value_grad = jnp.zeros((group_rows, HD), jnp.float32)
    for block_index in range(block_count):
        row_start = block_index * block_rows
        key_count = row_start + block_rows
        query_block = query_heads[head_index][row_start:key_count]
        key_rows = key_heads[head_index][:key_count]
        scores = block_scores(query_block, key_rows, row_start, key_count)
        probs = jnp.exp(scores - lse_heads[head_index][row_start:key_count])
        grad_block = d_attn[row_start:key_count]
        d_probs = jnp.einsum(
            "qd,kd->qk",
            grad_block,
            value_heads[head_index][:key_count],
            preferred_element_type=jnp.float32,
        )
        d_scores = (probs * (d_probs - jnp.sum(probs * d_probs, axis=1, keepdims=True))).astype(
            jnp.bfloat16
        )
        query_grads.append(
            jnp.dot(d_scores, key_rows, preferred_element_type=jnp.float32) * score_scale
        )
        key_grad = key_grad.at[:key_count].add(
            jnp.einsum("qk,qd->kd", d_scores, query_block, preferred_element_type=jnp.float32)
            * score_scale
        )
        value_grad = value_grad.at[:key_count].add(
            jnp.einsum(
                "qk,qd->kd",
                probs.astype(jnp.bfloat16),
                grad_block,
                preferred_element_type=jnp.float32,
            )
        )
    query_grad = rotate(jnp.concatenate(query_grads, axis=0), cosine_table, sine_table, -1.0)
    key_grad = rotate(key_grad, cosine_table, sine_table, -1.0)
    d_proj_heads = jnp.concatenate([query_grad, key_grad, value_grad], axis=1)
    d_proj = d_proj_heads.astype(jnp.bfloat16)
    qkv_bias_part = jnp.sum(d_proj, axis=0, dtype=jnp.float32).reshape(heads_here, 3 * HD)
    up_bias_part = jnp.sum(d_up, axis=0, dtype=jnp.float32)
    qkv_bias_grad, up_bias_grad = lax.psum((qkv_bias_part, up_bias_part), "dp")
    weight_piece = lax.all_gather(joined_in, "dp", axis=0, tiled=True)
    d_hidden = jnp.stack(
        (
            jnp.einsum(
                "gf,df->gd", d_proj, weight_piece[:, :qkv_cols], preferred_element_type=jnp.float32
            ),
            jnp.einsum(
                "gf,df->gd", d_up, weight_piece[:, qkv_cols:], preferred_element_type=jnp.float32
            ),
        )
    )
    d_first_part = d_hidden[0]
    d_second_part = d_hidden[1]
    grad_part = d_first_part * first_gain_f + d_second_part * second_gain_f
    grad_normed = lax.psum_scatter(
        grad_part.astype(jnp.bfloat16), "tensor", scatter_dimension=0, tiled=True
    ).astype(jnp.float32)
    shard_rows = width // lax.axis_size("dp")
    left_cols = first_all
    right_cols = second_all
    in_grad = lax.psum_scatter(
        jnp.concatenate(
            [
                jnp.einsum("gd,gf->df", left_cols, d_proj, preferred_element_type=jnp.float32),
                jnp.einsum("gd,gf->df", right_cols, d_up, preferred_element_type=jnp.float32),
            ],
            axis=1,
        ).astype(jnp.bfloat16),
        "dp",
        scatter_dimension=0,
        tiled=True,
    ).astype(jnp.float32)
    qkv_weight_grad = in_grad[:, :qkv_cols].reshape(shard_rows, heads_here, 3 * HD)
    up_weight_grad = in_grad[:, qkv_cols:]
    cot_cols = cot_all
    out_grad = (
        lax.psum_scatter(
            jnp.einsum("gd,gf->df", cot_cols, mixed, preferred_element_type=jnp.float32).astype(
                jnp.bfloat16
            ),
            "dp",
            scatter_dimension=0,
            tiled=True,
        )
        .astype(jnp.float32)
        .T
    )
    out_weight_grad = out_grad[:attn_cols]
    down_weight_grad = out_grad[attn_cols:]
    cot_values = cotangent.astype(jnp.float32)
    stat_terms = (
        jnp.sum(d_first_part * normed_all, axis=0),
        jnp.sum(d_first_part, axis=0),
        jnp.sum(d_second_part * normed_all, axis=0),
        jnp.sum(d_second_part, axis=0),
        jnp.sum(cot_values, axis=0),
    )
    first_gain_grad, first_shift_grad, second_gain_grad, second_shift_grad, bias_grad = lax.psum(
        (stat_terms[0], stat_terms[1], stat_terms[2], stat_terms[3], stat_terms[4]),
        ("dp", "tensor"),
    )
    layer_input_gradient = cot_values + inv_std * (
        grad_normed
        - jnp.mean(grad_normed, axis=1, keepdims=True)
        - normed * jnp.mean(grad_normed * normed, axis=1, keepdims=True)
    )
    return (
        output,
        layer_input_gradient,
        first_gain_grad,
        first_shift_grad,
        second_gain_grad,
        second_shift_grad,
        qkv_weight_grad,
        qkv_bias_grad,
        out_weight_grad,
        bias_grad,
        up_weight_grad,
        up_bias_grad,
        down_weight_grad,
        bias_grad,
    )


def solution(mesh):
    return jax.shard_map(
        body,
        mesh=mesh,
        in_specs=(
            P(("dp", "tensor"), None),
            P("dp", None),
            P(),
            P(),
            P(),
            P(),
            P("dp", "tensor", None),
            P("tensor", None),
            P("tensor", "dp"),
            P(),
            P("dp", "tensor"),
            P("tensor"),
            P("tensor", "dp"),
            P(),
            P(("dp", "tensor"), None),
        ),
        out_specs=(
            P(("dp", "tensor"), None),
            P(("dp", "tensor"), None),
            P(),
            P(),
            P(),
            P(),
            P("dp", "tensor", None),
            P("tensor", None),
            P("tensor", "dp"),
            P(),
            P("dp", "tensor"),
            P("tensor"),
            P("tensor", "dp"),
            P(),
        ),
        check_vma=False,
    )
```

profile of v0, /device:TPU:0, one launch (start us, length us, event | category | flops | bytes accessed | tf_op | source)
XLA Modules:
  0.0 931.6 jit_solution(4971245081132490845)
XLA Ops:
  7.2 2.9 pad_maximum_fusion.3
  11.0 1.3 fusion.50
  15.2 50.1 %all-gather.7.cloned.1.call-done = bf16[2048,1792]{1,0:T(8,128)(2,1)} async-done(((bf16[512,1792]{1,0:T(8,128)(2,1)}), bf16[2048,1792]{1,0:T(8,128)(2,1)}) %all-gather.7.cloned.1.call-update) | async-done | bytes 7340048 | tf_op jit(solution)/shard_map/all_gather | solution.py:99
  65.3 127.7 %all-gather.5.cloned.1.call-done = bf16[2048,2048]{1,0:T(8,128)(2,1)} async-done(((bf16[256,2048]{1,0:T(8,128)(2,1)}), bf16[2048,2048]{1,0:T(8,128)(2,1)}) %all-gather.5.cloned.1.call-update) | async-done | bytes 8388624 | tf_op jit(solution)/shard_map/all_gather | solution.py:90
  193.0 10.5 %fusion.156 = (bf16[2048,768]{0,1:T(8,128)(2,1)S(1)}, f32[2048,768]{0,1:T(8,128)S(1)}) fusion(f32[768]{0:T(1024)S(1)} %convert_reduce_fusion.5, bf16[2048,1792]{1,0:T(8,128)(2,1)} %all-gather.7.cloned.1.call-done, bf16[2048,2048]{1,0:T(8,128)(2,1)} %all-gather.5.cloned.1.call-done, f32[2048]{0:T(1024)S(1)} %convert_element_type.144, ...), kind=kOutput, calls=%fused_computation.244 | convolution fusion | flops 6462373888 | bytes 20990976 | tf_op jit(solution)/shard_map/dot_general | solution.py:102
  203.6 1.4 fusion.116
  209.1 1.4 fusion.158
  211.2 1.3 convolution_convert_fusion.3
  213.8 1.4 fusion.71
  215.3 1.6 fusion.72
  216.9 16.9 %all-gather.9.cloned.1.call-done = bf16[1280,2048]{1,0:T(8,128)(2,1)} async-done(((bf16[1280,512]{1,0:T(8,128)(2,1)}), bf16[1280,2048]{1,0:T(8,128)(2,1)}) %all-gather.9.cloned.1.call-update) | async-done | bytes 5242896 | tf_op jit(solution)/shard_map/all_gather | solution.py:161
  233.8 126.9 %all-gather.11.cloned.1.call-done = bf16[2048,2048]{1,0:T(8,128)(2,1)} async-done(((bf16[256,2048]{1,0:T(8,128)(2,1)}), bf16[2048,2048]{1,0:T(8,128)(2,1)}) %all-gather.11.cloned.1.call-update) | async-done | bytes 8388624 | tf_op jit(solution)/shard_map/all_gather | solution.py:170
  360.7 17.0 %fusion.157 = (bf16[2048,1280]{1,0:T(8,128)(2,1)S(1)}, f32[2048,1280]{1,0:T(8,128)}) fusion(bf16[1280,2048]{1,0:T(8,128)(2,1)} %all-gather.9.cloned.1.call-done, bf16[2048,2048]{1,0:T(8,128)(2,1)} %all-gather.11.cloned.1.call-done), kind=kOutput, calls=%fused_computation.245 | convolution fusion | flops 10740039680 | bytes 29360128 | tf_op jit(solution)/shard_map/gd,fd->gf/dot_general | solution.py:172
  378.8 2.7 convolution_multiply_fusion.9
  381.5 1.6 scatter-add.20
  383.1 1.5 scatter-add.25
  385.8 1.3 convolution_multiply_fusion.6
  388.7 1.4 convolution_multiply_fusion.7
  393.3 1.5 convolution_multiply_fusion.5
  395.6 33.6 %convert_reduce_fusion = (f32[1024]{0:T(1024)S(1)}, bf16[2048,1024]{1,0:T(8,128)(2,1)}, f32[2048,1024]{1,0:T(8,128)}, f32[2048,1024]{1,0:T(8,128)}) fusion(f32[2048,1280]{1,0:T(8,128)} %get-tuple-element.190, f32[1024]{0:T(1024)S(1)} %convert_element_type.158, bf16[2048,1792]{1,0:T(8,128)(2,1)} %all-gather.7.cloned.1.call-done, ...), kind=kOutput, calls=%fused_computation.14 | convolution fusion | flops 8763997184 | bytes 41967616 | tf_op jit(solution)/shard_map/dot_general | solution.py:103
  429.2 10.2 %multiply_convert_fusion = bf16[2048,1024]{1,0:T(8,128)(2,1)} fusion(f32[2048,1024]{1,0:T(8,128)} %get-tuple-element.169, f32[2048,1024]{1,0:T(8,128)} %get-tuple-element.186, f32[1024]{0:T(1024)S(1)} %convert_element_type.158), kind=kLoop, calls=%fused_computation.16 | loop fusion | flops 8388608 | bytes 20975616 | tf_op jit(solution)/shard_map/convert_element_type | solution.py:157
  439.4 16.6 %fusion.12 = bf16[2048,1280]{0,1:T(8,128)(2,1)} fusion(bf16[2048,2048]{1,0:T(8,128)(2,1)} %all-gather.11.cloned.1.call-done, bf16[2048,1024]{1,0:T(8,128)(2,1)} %multiply_convert_fusion, bf16[512,256]{1,0:T(8,128)(2,1)S(1)} %copy-done.60, bf16[512,256]{1,0:T(8,128)(2,1)S(1)} %copy-done.58, bf16[512,256]{1,0:T(8,128)(2,1)S(1)} %copy-done.57, ...), kind=kOutput, calls=%fused_computation.33 | convolution fusion | flops 10766254080 | bytes 18874368 | tf_op jit(solution)/shard_map/gd,gf->df/dot_general | solution.py:261
  457.0 1.5 convolution_multiply_fusion.8
  458.5 2.8 pad_maximum_fusion.2
  461.3 2.4 fusion.68
  463.7 1.9 fusion.69
  467.2 2.1 fusion.39
  469.3 1.4 fusion.149
  474.4 2.0 fusion.46
  476.4 8.2 fusion.30
  484.6 10.1 %fusion.22 = bf16[2048,1024]{0,1:T(8,128)(2,1)S(1)} fusion(bf16[2048,1024]{1,0:T(8,128)(2,1)S(1)} %copy-done.59, bf16[2048,2048]{1,0:T(8,128)(2,1)S(1)} %bitcast.51, f32[2048]{0:T(1024)S(1)} %convert_element_type.156, f32[2048]{0:T(1024)S(1)} %convert_element_type.155), kind=kOutput, calls=%fused_computation.48 | convolution fusion | flops 8608808960 | bytes 16793600 | tf_op jit(solution)/shard_map/gd,gf->df/dot_general | solution.py:248
  494.7 5.9 pad_maximum_fusion
  500.7 1.8 copy-done.26
  502.5 13.3 %fusion.41 = f32[2048,2048]{1,0:T(8,128)} fusion(bf16[2048,768]{0,1:T(8,128)(2,1)S(1)} %copy-done.26, bf16[2048,1792]{1,0:T(8,128)(2,1)} %all-gather.7.cloned.1.call-done), kind=kOutput, calls=%fused_computation.75 | convolution fusion | flops 6442450944 | bytes 23068672 | tf_op jit(solution)/shard_map/gf,df->gd/dot_general | solution.py:227
  515.8 25.9 %fusion.151 = (f32[2048]{0:T(1024)S(1)}, f32[2048]{0:T(1024)S(1)}, bf16[2048,2048]{1,0:T(8,128)(2,1)}, f32[2048]{0:T(1024)S(1)}, f32[2048]{0:T(1024)S(1)}) fusion(bf16[2048,2048]{1,0:T(8,128)(2,1)} %all-gather.5.cloned.1.call-done, f32[2048]{0:T(1024)S(1)} %convert_element_type.155, f32[2048,2048]{1,0:T(8,128)} %fusion.41, f32[2048]{0:T(1024)S(1)} %copy-done.44, ...), kind=kOutput, calls=%fused_computation.240 | convolution fusion | flops 8636063744 | bytes 41992192 | tf_op jit(solution)/shard_map/gf,df->gd/dot_general | solution.py:230
  541.7 17.3 %convolution_convert_fusion = bf16[2048,2048]{1,0:T(8,128)(2,1)} fusion(bf16[1280,2048]{1,0:T(8,128)(2,1)} %all-gather.9.cloned.1.call-done, bf16[2048,1024]{1,0:T(8,128)(2,1)} %multiply_convert_fusion, bf16[512,256]{1,0:T(8,128)(2,1)} %fusion.72, bf16[512,256]{1,0:T(8,128)(2,1)} %fusion.71, bf16[512,256]{1,0:T(8,128)(2,1)} %convolution_convert_fusion.2, ...), kind=kOutput, calls=%fused_computation.30 | convolution fusion | flops 10767826944 | bytes 18874368 | tf_op jit(solution)/shard_map/dot_general | solution.py:159
  560.3 7.0 all-reduce.3
  567.3 1.7 convert_bitcast_fusion
  569.8 1.5 slice.435
  571.3 2.8 reduce-scatter.9.cloned.1.call-done
  574.1 3.0 slice.434
  577.1 2.9 copy.42
  580.6 2.8 copy.41
  583.4 143.4 %reduce-scatter.7.cloned.1.call-done = bf16[256,2048]{1,0:T(8,128)(2,1)} async-done(((bf16[2048,2048]{1,0:T(8,128)(2,1)}), bf16[256,2048]{1,0:T(8,128)(2,1)}) %reduce-scatter.7.cloned.1.call-update) | async-done | bytes 1048592 | tf_op jit(solution)/shard_map/reduce_scatter | solution.py:238
  726.7 1.9 convert_reduce_fusion.2
  728.7 150.1 %reduce-scatter.5.cloned.1.call-done = bf16[256,2048]{1,0:T(8,128)(2,1)} async-done(((bf16[2048,2048]{1,0:T(8,128)(2,1)}), bf16[256,2048]{1,0:T(8,128)(2,1)}) %reduce-scatter.5.cloned.1.call-update) | async-done | bytes 1048592 | tf_op jit(solution)/shard_map/reduce_scatter | solution.py:164
  878.8 4.9 convert_reduce_fusion.4
  883.7 40.3 %all-reduce.2 = (f32[2048]{0:T(1024)}, f32[2048]{0:T(1024)}, f32[2048]{0:T(1024)}, f32[2048]{0:T(1024)}, f32[2048]{0:T(1024)S(1)}) all-reduce(f32[2048]{0:T(1024)S(1)} %get-tuple-element.171, f32[2048]{0:T(1024)S(1)} %get-tuple-element.172, f32[2048]{0:T(1024)S(1)} %get-tuple-element.155, ...), channel_id=1, replica_groups=mesh['dp'=4,'tensor'=8] {'dp','tensor'}, use_global_device_ids=true, to_apply=%region_21.22 | all-reduce | flops 10240 | bytes 81920 | tf_op jit(solution)/shard_map/psum | solution.py:281
  (218 shorter events, 26.7 us)
Async XLA Ops:
  7.2 58.1 %all-gather.7.cloned.1.call-start = ((), (), s32[]{:S(2)}) async-start(), calls=%async_computation.5 | async-start | bytes 9175040 | tf_op jit(solution)/shard_map/all_gather | solution.py:99
  10.1 182.8 %all-gather.5.cloned.1.call-start = ((), (), s32[]{:S(2)}) async-start(), calls=%async_computation.4 | async-start | bytes 9437184 | tf_op jit(solution)/shard_map/all_gather | solution.py:90
  10.4 3.7 copy-start.37
  10.9 3.4 copy-start.36
  10.9 4.2 copy-start.54
  11.0 192.5 %copy-start.39 = (f32[256]{0:T(256)}, f32[256]{0:T(256)S(1)}, u32[]{:S(2)}) copy-start(f32[256]{0:T(256)S(1)} %add_rsqrt_fusion) | copy-start | bytes 3076
  12.3 221.5 %all-gather.9.cloned.1.call-start = ((), (), s32[]{:S(2)}) async-start(), calls=%async_computation.6 | async-start | bytes 6553600 | tf_op jit(solution)/shard_map/all_gather | solution.py:161
  13.5 347.2 %all-gather.11.cloned.1.call-start = ((), (), s32[]{:S(2)}) async-start(), calls=%async_computation.8 | async-start | bytes 9437184 | tf_op jit(solution)/shard_map/all_gather | solution.py:170
  14.1 553.2 %reduce-scatter.11.cloned.1.call-start = ((), (), s32[]{:S(2)}) async-start(), calls=%async_computation.11 | async-start | bytes 6553600 | tf_op jit(solution)/shard_map/reduce_scatter | solution.py:260
  14.2 189.3 %copy-start.43 = (f32[2048]{0:T(1024)}, f32[2048]{0:T(1024)S(1)}, u32[]{:S(2)}) copy-start(f32[2048]{0:T(1024)S(1)} %convert_element_type.143) | copy-start | bytes 24580
  14.3 189.3 %copy-start.45 = (f32[2048]{0:T(1024)}, f32[2048]{0:T(1024)S(1)}, u32[]{:S(2)}) copy-start(f32[2048]{0:T(1024)S(1)} %convert_element_type.144) | copy-start | bytes 24580
  14.9 188.6 %copy-start.41 = (f32[32]{0:T(128)}, f32[32]{0:T(128)S(1)}, u32[]{:S(2)}) copy-start(f32[32]{0:T(128)S(1)} %multiply_power_fusion) | copy-start | bytes 388
  15.2 188.3 %copy-start.33 = (f32[2048]{0:T(1024)}, f32[2048]{0:T(1024)S(1)}, u32[]{:S(2)}) copy-start(f32[2048]{0:T(1024)S(1)} %fusion.150) | copy-start | bytes 24580
  203.5 11.7 %copy-start.19 = (bf16[2048,768]{0,1:T(8,128)(2,1)}, bf16[2048,768]{0,1:T(8,128)(2,1)S(1)}, u32[]{:S(2)}) copy-start(bf16[2048,768]{0,1:T(8,128)(2,1)S(1)} %get-tuple-element.187) | copy-start | bytes 9437188
  205.1 3.9 copy-start.15
  205.4 3.6 copy-start.22
  205.9 5.3 copy-start.10
  206.8 5.7 copy-start.3
  210.5 4.8 copy-start
  360.7 17.0 %copy-start.11 = (f32[512,512]{0,1:T(8,128)S(1)}, f32[512,512]{0,1:T(8,128)}, u32[]{:S(2)}) copy-start(f32[512,512]{0,1:T(8,128)} %copy-done.10) | copy-start | bytes 3145732
  360.7 17.4 %copy-start.20 = (bf16[2048,768]{0,1:T(8,128)(2,1)S(1)}, bf16[2048,768]{0,1:T(8,128)(2,1)}, u32[]{:S(2)}) copy-start(bf16[2048,768]{0,1:T(8,128)(2,1)} %copy-done.19) | copy-start | bytes 9437188
  377.7 12.4 %copy-start.32 = (bf16[2048,1280]{1,0:T(8,128)(2,1)}, bf16[2048,1280]{1,0:T(8,128)(2,1)S(1)}, u32[]{:S(2)}) copy-start(bf16[2048,1280]{1,0:T(8,128)(2,1)S(1)} %get-tuple-element.189) | copy-start | bytes 15728644
  378.5 6.1 copy-start.4
  378.8 6.4 copy-start.21
  390.9 3.9 slice-start.1
  392.1 3.5 slice-start.2
  393.3 35.8 %copy-start.13 = (bf16[512,2048]{1,0:T(8,128)(2,1)}, bf16[512,2048]{1,0:T(8,128)(2,1)S(1)}, u32[]{:S(2)}) copy-start(bf16[512,2048]{1,0:T(8,128)(2,1)S(1)} %multiply_convert_fusion.1) | copy-start | bytes 6291460
  429.1 10.2 %copy-start.56 = (bf16[512,256]{1,0:T(8,128)(2,1)S(1)}, bf16[512,256]{1,0:T(8,128)(2,1)}, u32[]{:S(2)}) copy-start(bf16[512,256]{1,0:T(8,128)(2,1)} %convolution_convert_fusion.3) | copy-start | bytes 786436
  429.1 10.2 %copy-start.57 = (bf16[512,256]{1,0:T(8,128)(2,1)S(1)}, bf16[512,256]{1,0:T(8,128)(2,1)}, u32[]{:S(2)}) copy-start(bf16[512,256]{1,0:T(8,128)(2,1)} %convolution_convert_fusion.2) | copy-start | bytes 786436
  429.1 10.2 %copy-start.58 = (bf16[512,256]{1,0:T(8,128)(2,1)S(1)}, bf16[512,256]{1,0:T(8,128)(2,1)}, u32[]{:S(2)}) copy-start(bf16[512,256]{1,0:T(8,128)(2,1)} %fusion.71) | copy-start | bytes 786436
  429.1 10.2 %copy-start.60 = (bf16[512,256]{1,0:T(8,128)(2,1)S(1)}, bf16[512,256]{1,0:T(8,128)(2,1)}, u32[]{:S(2)}) copy-start(bf16[512,256]{1,0:T(8,128)(2,1)} %fusion.72) | copy-start | bytes 786436
  456.0 118.0 %reduce-scatter.9.cloned.1.call-start = ((), (), s32[]{:S(2)}) async-start(), calls=%async_computation.10 | async-start | bytes 9175040 | tf_op jit(solution)/shard_map/reduce_scatter | solution.py:244
  457.0 4.3 copy-start.8
  457.0 6.7 copy-start.5
  457.0 6.7 copy-start.9
  461.3 4.4 copy-start.18
  461.3 4.4 copy-start.23
  467.2 9.2 slice-start.3
  469.3 5.1 copy-start.2
  471.9 4.4 slice-start.4
  476.4 8.2 copy-start.25
  476.4 8.2 copy-start.59
  500.6 226.1 %reduce-scatter.7.cloned.1.call-start = ((), (), s32[]{:S(2)}) async-start(), calls=%async_computation.9 | async-start | bytes 9437184 | tf_op jit(solution)/shard_map/reduce_scatter | solution.py:238
  541.7 337.2 %reduce-scatter.5.cloned.1.call-start = ((), (), s32[]{:S(2)}) async-start(), calls=%async_computation.7 | async-start | bytes 9437184 | tf_op jit(solution)/shard_map/reduce_scatter | solution.py:164
  574.1 5.9 copy-start.12
  580.5 146.3 %copy-start.7 = (bf16[256,2048]{1,0:T(8,128)(2,1)S(1)}, bf16[256,2048]{1,0:T(8,128)(2,1)}, u32[]{:S(2)}) copy-start(bf16[256,2048]{1,0:T(8,128)(2,1)} %param.35) | copy-start | bytes 3145732
  580.5 146.3 %copy-start.38 = (f32[256]{0:T(256)S(1)}, f32[256]{0:T(256)}, u32[]{:S(2)}) copy-start(f32[256]{0:T(256)} %copy-done.37) | copy-start | bytes 3076
  580.5 146.3 %copy-start.40 = (f32[256]{0:T(256)S(1)}, f32[256]{0:T(256)}, u32[]{:S(2)}) copy-start(f32[256]{0:T(256)} %copy-done.39) | copy-start | bytes 3076
  (26 other events, 55.4 us)
Sparse Core Ops, SparseCore 0:
  10.3 55.0 all-gather.6
  68.0 124.9 all-gather.4
  195.1 38.6 all-gather.8
  235.8 124.9 all-gather.10
  456.2 49.5 reduce-scatter.10
  508.3 65.7 reduce-scatter.8
  577.7 148.9 reduce-scatter.6
  730.8 147.9 reduce-scatter.4
where the time goes:
time: 937 us; the launch traced here: 932 us
  waiting for transfers between devices  619 us (66%)
  matrix products  183 us (20%)
  blocking collectives  47.3 us (5%)
  other arithmetic  45.8 us (5%)
  local copies, waits for them, and re-layouts  20.9 us (2%)
  between operations  15.5 us (2%)
    reduce_scatter x1, waiting for transfers between devices, body(): lax.psum_scatter(incomplete_sum.astype(jnp.bfloat16), 'tensor', scatter_d...  150 us
    reduce_scatter x1, waiting for transfers between devices, body(): lax.psum_scatter(grad_part.astype(jnp.bfloat16), 'tensor', scatter_dimens...  143 us
    all_gather x1, waiting for transfers between devices, body(): lax.all_gather(normed_local, 'tensor', axis=0, tiled=True)  128 us
    all_gather x1, waiting for transfers between devices, body(): cot_all = lax.all_gather(cotangent, 'tensor', axis=0, tiled=True)  127 us
    all_gather x1, waiting for transfers between devices, body(): weight_piece = lax.all_gather(joined_in, 'dp', axis=0, tiled=True)  50.1 us
    psum x1, blocking collectives, body(): lax.psum((stat_terms[0], stat_terms[1], stat_terms[2], stat_terms[3], sta...  40.3 us
    dot_general x1, matrix products, body(): jnp.dot(right_cols, weight_piece[:, qkv_cols:], preferred_element_type=jn...  33.6 us
    dot_general x1, matrix products, body(): jnp.einsum('gf,df->gd', d_up, weight_piece[:, qkv_cols:], preferred_eleme...  25.9 us
  transfers between devices with their start and end apart: 8, of which 7 were waited for; matrix products, arithmetic and copies ran while one was open for 15% of the time, Pallas kernels for 0%

commit v1 on v0

v1 whole, which is shorter than its diff:
```python
import math

import jax
import jax.numpy as jnp
from jax import lax
from jax.sharding import PartitionSpec as P

HD = 256
ROT = 64

NORM_EPS = 1e-05
MASK_FILL = -1e30
F32 = jnp.float32
BF16 = jnp.bfloat16


def normalize(values):
    mean_val = jnp.mean(values, axis=-1, keepdims=True)
    centred = values - mean_val
    spread = jnp.mean(centred * centred, axis=-1, keepdims=True)
    inv_std = lax.rsqrt(spread + NORM_EPS)
    return (centred * inv_std, inv_std)


def positions_of(segment):
    row_count = segment.shape[0]
    position_index = jnp.arange(row_count, dtype=jnp.int32)
    starts = jnp.concatenate([jnp.ones((1,), dtype=jnp.bool_), segment[1:] != segment[:-1]])
    first_index = lax.cummax(
        jnp.where(starts, position_index, jnp.zeros_like(position_index)), axis=0
    )
    return position_index - first_index


def rotation_tables(position):
    half_dims = ROT // 2
    inv_freq = 10000.0 ** (-2.0 * jnp.arange(half_dims, dtype=jnp.float32) / ROT)
    angles = position.astype(jnp.float32)[:, None] * inv_freq[None, :]
    return (jnp.cos(angles), jnp.sin(angles))


def rotate(values, cosine_table, sine_table, direction):
    half_dims = ROT // 2
    leading = values[:, :half_dims]
    trailing = values[:, half_dims:ROT]
    return jnp.concatenate(
        [
            leading * cosine_table - direction * trailing * sine_table,
            trailing * cosine_table + direction * leading * sine_table,
            values[:, ROT:],
        ],
        axis=1,
    )


def after(value, *others):
    return lax.optimization_barrier((value,) + others)[0]


class Ring:
    def __init__(self, axis):
        self.axis = axis
        size = lax.axis_size(axis)
        order = list(range(0, size, 2)) + list(range(size - 1, 0, -2))
        self.size = size
        self.order = jnp.array(order, jnp.int32)
        place = [order.index(i) for i in range(size)]
        self.place = jnp.array(place, jnp.int32)[lax.axis_index(axis)]
        self.up = [(order[i], order[(i + 1) % size]) for i in range(size)]
        self.down = [(order[i], order[(i - 1) % size]) for i in range(size)]

    def index(self, offset):
        return self.order[(self.place + offset) % self.size]

    def send_up(self, value):
        return lax.ppermute(value, self.axis, self.up)

    def send_down(self, value):
        return lax.ppermute(value, self.axis, self.down)

    def gather(self, block):
        half = block.shape[0] // 2
        got = [(0, block)]
        up = down = block
        for step in range(1, self.size // 2):
            up, down = self.send_up(up), self.send_down(down)
            got += [(-step, up), (step, down)]
        far = jnp.concatenate([self.send_up(up[:half]), self.send_down(down[half:])], axis=0)
        got.append((self.size // 2, far))
        return got, (up, down)

    def place_rows(self, got):
        rows, cols = got[0][1].shape
        whole = jnp.zeros((rows * self.size, cols), got[0][1].dtype)
        for offset, block in got:
            whole = lax.dynamic_update_slice(whole, block, (self.index(offset) * rows, 0))
        return whole

    def scatter_sum(self, part, rows, cols, pieces):
        half, width = rows // 2, cols // pieces
        result = []
        far = self.size // 2
        for piece in range(pieces):
            window = (piece * width, width)
            arrived = []
            for send, sign, start in ((self.send_up, 1, 0), (self.send_down, -1, half)):
                first = self.index(sign * far) * rows + start
                moving = send(part(first, half, window).astype(BF16)).astype(F32)
                for step in range(far - 1, 0, -1):
                    own = part(self.index(sign * step) * rows, rows, window)
                    if step == far - 1:
                        pad = ((0, rows - half), (0, 0)) if start == 0 else ((half, 0), (0, 0))
                        moving = jnp.pad(moving, pad)
                    moving = send((own + moving).astype(BF16)).astype(F32)
                arrived.append(moving)
            own = part(self.index(0) * rows, rows, window)
            result.append(own + arrived[0] + arrived[1])
        return jnp.concatenate(result, axis=1)


def doubling_sum(value, axis):
    size = lax.axis_size(axis)
    step = 1
    while step < size:
        value = value + lax.ppermute(value, axis, [(i, i ^ step) for i in range(size)])
        step *= 2
    return value


def doubling_gather(value, axis):
    size = lax.axis_size(axis)
    me = lax.axis_index(axis)
    step = 1
    while step < size:
        other = lax.ppermute(value, axis, [(i, i ^ step) for i in range(size)])
        upper = (me & step) != 0
        value = jnp.where(
            upper,
            jnp.concatenate([other, value], axis=1),
            jnp.concatenate([value, other], axis=1),
        )
        step *= 2
    return value


def body(
    tokens,
    segment_ids,
    first_gain,
    first_shift,
    second_gain,
    second_shift,
    qkv_weight,
    qkv_bias,
    out_weight,
    out_bias,
    up_projection_weight,
    up_bias,
    down_weight,
    down_bias,
    cotangent,
):
    width = tokens.shape[1]
    rows = tokens.shape[0]
    qkv_cols = 3 * HD
    segment = segment_ids[0]
    group_rows = segment.shape[0]
    block_rows = min(512, group_rows)
    block_count = group_rows // block_rows
    ring = Ring("tensor")
    shard_rows = qkv_weight.shape[0]
    dp_start = lax.axis_index("dp") * shard_rows

    w_qkv = qkv_weight.reshape(shard_rows, qkv_cols).astype(F32)
    w_up = up_projection_weight.astype(F32)

    def shard(vector):
        return lax.dynamic_slice(vector, (dp_start,), (shard_rows,)).astype(F32)

    gain1, gain2 = shard(first_gain), shard(second_gain)
    shift1, shift2 = shard(first_shift), shard(second_shift)
    scaled = jnp.concatenate(
        [w_qkv * gain1[:, None], w_up * gain2[:, None]], axis=1
    ).astype(BF16)
    w_in = lax.all_gather(scaled, "dp", axis=0, tiled=True)
    shift_part = jnp.concatenate(
        [jnp.sum(w_qkv * shift1[:, None], axis=0), jnp.sum(w_up * shift2[:, None], axis=0)]
    )
    in_bias = doubling_sum(shift_part[None], "dp")[0] + jnp.concatenate(
        [qkv_bias.reshape(-1), up_bias]
    ).astype(F32)
    w_out = lax.all_gather(
        jnp.concatenate([out_weight, down_weight], axis=0), "dp", axis=1, tiled=True
    )

    x_values = tokens.astype(F32)
    normed, inv_std = normalize(x_values)
    token_blocks, token_last = ring.gather(normed.astype(BF16))
    normed_all = ring.place_rows(token_blocks)
    cot_blocks, cot_last = ring.gather(after(cotangent, token_last[0], token_last[1]))
    cot_all = ring.place_rows(cot_blocks)

    position = positions_of(segment)
    cosine_table, sine_table = rotation_tables(position)
    position_index = jnp.arange(group_rows, dtype=jnp.int32)
    score_scale = 1.0 / math.sqrt(HD)

    proj = (
        jnp.dot(normed_all, w_in[:, :qkv_cols], preferred_element_type=F32)
        + in_bias[None, :qkv_cols]
    )
    query = rotate(proj[:, :HD], cosine_table, sine_table, 1.0).astype(BF16)
    key = rotate(proj[:, HD : 2 * HD], cosine_table, sine_table, 1.0).astype(BF16)
    value = proj[:, 2 * HD :].astype(BF16)
    up = (
        jnp.dot(normed_all, w_in[:, qkv_cols:], preferred_element_type=F32)
        + in_bias[None, qkv_cols:]
    )
    cdf = 0.5 * (1.0 + lax.erf(up * (1.0 / math.sqrt(2.0))))
    act = (up * cdf).astype(BF16)
    slope = (cdf + up * (jnp.exp(-0.5 * up * up) * (1.0 / math.sqrt(2.0 * math.pi)))).astype(BF16)

    def block_scores(row_start, key_count):
        raw = (
            jnp.einsum(
                "qd,kd->qk",
                query[row_start:key_count],
                key[:key_count],
                preferred_element_type=F32,
            )
            * score_scale
        )
        seg_query = segment[row_start:key_count]
        allowed = (seg_query[:, None] == segment[None, :key_count]) & (
            position_index[row_start:key_count, None] >= position_index[None, :key_count]
        )
        return jnp.where(allowed, raw, MASK_FILL)

    rows_out = []
    lse_rows = []
    for block_index in range(block_count):
        row_start = block_index * block_rows
        key_count = row_start + block_rows
        scores = block_scores(row_start, key_count)
        row_top = jnp.max(scores, axis=1, keepdims=True)
        exp_scores = jnp.exp(scores - row_top)
        row_total = jnp.sum(exp_scores, axis=1, keepdims=True)
        probs_low = (exp_scores / row_total).astype(BF16)
        rows_out.append(
            jnp.dot(probs_low, value[:key_count], preferred_element_type=F32).astype(BF16)
        )
        lse_rows.append(row_top + jnp.log(row_total))
    attn = jnp.concatenate(rows_out, axis=0)
    lse = jnp.concatenate(lse_rows, axis=0)
    mixed = jnp.concatenate([attn, act], axis=1)

    mixed_out = after(mixed, cot_last[0], cot_last[1])

    def out_part(first, count, window):
        block = lax.dynamic_slice(mixed_out, (first, 0), (count, mixed.shape[1]))
        return jnp.dot(
            block, w_out[:, window[0] : window[0] + window[1]], preferred_element_type=F32
        )

    summed = ring.scatter_sum(out_part, rows, width, 2)
    output = (x_values + out_bias.astype(F32) + down_bias.astype(F32) + summed).astype(BF16)

    back_mixed = jnp.einsum("gd,fd->gf", cot_all, w_out, preferred_element_type=F32)
    d_attn = back_mixed[:, :HD].astype(BF16)
    d_up = (back_mixed[:, HD:] * slope.astype(F32)).astype(BF16)
    query_grads = []
    key_grad = jnp.zeros((group_rows, HD), F32)
    value_grad = jnp.zeros((group_rows, HD), F32)
    for block_index in range(block_count):
        row_start = block_index * block_rows
        key_count = row_start + block_rows
        scores = block_scores(row_start, key_count)
        probs = jnp.exp(scores - lse[row_start:key_count])
        grad_block = d_attn[row_start:key_count]
        d_probs = jnp.einsum(
            "qd,kd->qk", grad_block, value[:key_count], preferred_element_type=F32
        )
        d_scores = (probs * (d_probs - jnp.sum(probs * d_probs, axis=1, keepdims=True))).astype(
            BF16
        )
        query_grads.append(
            jnp.dot(d_scores, key[:key_count], preferred_element_type=F32) * score_scale
        )
        key_grad = key_grad.at[:key_count].add(
            jnp.einsum(
                "qk,qd->kd", d_scores, query[row_start:key_count], preferred_element_type=F32
            )
            * score_scale
        )
        value_grad = value_grad.at[:key_count].add(
            jnp.einsum("qk,qd->kd", probs.astype(BF16), grad_block, preferred_element_type=F32)
        )
    query_grad = rotate(jnp.concatenate(query_grads, axis=0), cosine_table, sine_table, -1.0)
    key_grad = rotate(key_grad, cosine_table, sine_table, -1.0)
    d_proj = jnp.concatenate([query_grad, key_grad, value_grad], axis=1).astype(BF16)
    d_in = jnp.concatenate([d_proj, d_up], axis=1)

    def grad_piece(first, count, window):
        block = lax.dynamic_slice(d_in, (first, 0), (count, d_in.shape[1]))
        return jnp.einsum(
            "gf,df->gd",
            block,
            w_in[window[0] : window[0] + window[1]],
            preferred_element_type=F32,
        )

    grad_normed = ring.scatter_sum(grad_piece, rows, width, 2)
    cot_values = cotangent.astype(F32)
    layer_input_gradient = cot_values + inv_std * (
        grad_normed
        - jnp.mean(grad_normed, axis=1, keepdims=True)
        - normed * jnp.mean(grad_normed * normed, axis=1, keepdims=True)
    )

    out_grad = lax.psum_scatter(
        jnp.einsum("gd,gf->df", cot_all, mixed, preferred_element_type=F32).astype(BF16),
        "dp",
        scatter_dimension=0,
        tiled=True,
    )
    out_grad = out_grad.astype(F32).T
    raw_in = lax.psum_scatter(
        jnp.einsum("gd,gf->df", normed_all, d_in, preferred_element_type=F32).astype(BF16),
        "dp",
        scatter_dimension=0,
        tiled=True,
    ).astype(F32)
    in_sum = doubling_sum(jnp.sum(d_in, axis=0, dtype=F32)[None], "dp")[0]
    qkv_sum, up_sum = in_sum[:qkv_cols], in_sum[qkv_cols:]
    raw_qkv, raw_up = raw_in[:, :qkv_cols], raw_in[:, qkv_cols:]
    qkv_weight_grad = raw_qkv * gain1[:, None] + shift1[:, None] * qkv_sum[None]
    up_weight_grad = raw_up * gain2[:, None] + shift2[:, None] * up_sum[None]
    stats = jnp.stack(
        [
            jnp.sum(w_qkv * raw_qkv, axis=1),
            jnp.sum(w_qkv * qkv_sum[None], axis=1),
            jnp.sum(w_up * raw_up, axis=1),
            jnp.sum(w_up * up_sum[None], axis=1),
        ]
    )
    stats = doubling_gather(doubling_sum(stats, "tensor"), "dp")
    bias_grad = doubling_sum(
        doubling_sum(jnp.sum(cot_values, axis=0)[None], "tensor"), "dp"
    )[0]
    return (
        output,
        layer_input_gradient,
        stats[0],
        stats[1],
        stats[2],
        stats[3],
        qkv_weight_grad.reshape(shard_rows, 1, qkv_cols),
        qkv_sum.reshape(1, qkv_cols),
        out_grad[:HD],
        bias_grad,
        up_weight_grad,
        up_sum,
        out_grad[HD:],
        bias_grad,
    )


def solution(mesh):
    return jax.shard_map(
        body,
        mesh=mesh,
        in_specs=(
            P(("dp", "tensor"), None),
            P("dp", None),
            P(),
            P(),
            P(),
            P(),
            P("dp", "tensor", None),
            P("tensor", None),
            P("tensor", "dp"),
            P(),
            P("dp", "tensor"),
            P("tensor"),
            P("tensor", "dp"),
            P(),
            P(("dp", "tensor"), None),
        ),
        out_specs=(
            P(("dp", "tensor"), None),
            P(("dp", "tensor"), None),
            P(),
            P(),
            P(),
            P(),
            P("dp", "tensor", None),
            P("tensor", None),
            P("tensor", "dp"),
            P(),
            P("dp", "tensor"),
            P("tensor"),
            P("tensor", "dp"),
            P(),
        ),
        check_vma=False,
    )
```

time: 937 us -> 598 us (0.64)
  waiting for transfers between devices: 619 us -> 233 us
  starting transfers between devices: 0.33 us -> 68.2 us
  blocking collectives: 47.3 us -> 0 us
  local copies, waits for them, and re-layouts: 20.9 us -> 48.1 us
  between operations: 15.5 us -> 29 us
  matrix products: 183 us -> 172 us
    all_gather x4 -> x2, waiting for transfers between devices: 322 us -> 0.01 us  [the longest x1 0.01 us: body(): lax.all_gather(jnp.concatenate([out_weight, down_weight], axis=0), 'dp',...]
    reduce_scatter x4 -> x2, waiting for transfers between devices: 296 us -> 0.01 us  [the longest x1 0.01 us: body(): lax.psum_scatter(jnp.einsum('gd,gf->df', normed_all, d_in, preferred_elem...]
    ppermute x0 -> x62, waiting for transfers between devices: none -> 233 us  [the longest x24 182 us: send_up(): return lax.ppermute(value, self.axis, self.up)]
    ppermute x0 -> x62, starting transfers between devices: none -> 67.8 us  [the longest x24 35.3 us: send_up(): return lax.ppermute(value, self.axis, self.up)]
    psum x2 -> x0, blocking collectives: 47.3 us -> none  [the longest x1 40.3 us: body(): lax.psum((stat_terms[0], stat_terms[1], stat_terms[2], stat_terms[3], sta...]
    dynamic_update_slice x0 -> x13, local copies, waits for them, and re-layouts: none -> 21.5 us  [place_rows(): lax.dynamic_update_slice(whole, block, (self.index(offset) * rows, 0))]
    dot_general x33 -> x65, matrix products: 183 us -> 172 us  [the longest x18 33.6 us: grad_piece(): jnp.einsum('gf,df->gd', block, w_in[window[0]:window[0] + window[1]], pre...]
  transfers between devices with their start and end apart: 8 -> 66, of which waited for: 7 -> 29; matrix products, arithmetic and copies ran while one was open for 15% -> 28% of each run, Pallas kernels for 0% -> 0%
where the time goes in v1:
time: 598 us; the launch traced here: 591 us
  waiting for transfers between devices  233 us (39%)
  matrix products  172 us (29%)
  starting transfers between devices  68.2 us (11%)
  local copies, waits for them, and re-layouts  48.1 us (8%)
  other arithmetic  41.8 us (7%)
  between operations  29 us (5%)
    ppermute x24, waiting for transfers between devices, send_up(): return lax.ppermute(value, self.axis, self.up)  182 us
    ppermute x24, waiting for transfers between devices, send_down(): return lax.ppermute(value, self.axis, self.down)  40.7 us
    ppermute x24, starting transfers between devices, send_up(): return lax.ppermute(value, self.axis, self.up)  35.3 us
    dot_general x18, matrix products, grad_piece(): jnp.einsum('gf,df->gd', block, w_in[window[0]:window[0] + window[1]], pre...  33.6 us
    dot_general x18, matrix products, out_part(): jnp.dot(block, w_out[:, window[0]:window[0] + window[1]], preferred_eleme...  25.9 us
    dynamic_update_slice x13, local copies, waits for them, and re-layouts, place_rows(): lax.dynamic_update_slice(whole, block, (self.index(offset) * rows, 0))  21.5 us
    dot_general x1, matrix products, body(): jnp.einsum('gd,gf->df', normed_all, d_in, preferred_element_type=F32)  21.1 us
    dot_general x1, matrix products, body(): jnp.dot(normed_all, w_in[:, qkv_cols:], preferred_element_type=F32)  19.8 us
  transfers between devices with their start and end apart: 66, of which 29 were waited for; matrix products, arithmetic and copies ran while one was open for 28% of the time, Pallas kernels for 0%

profile of v1, /device:TPU:0, one launch (start us, length us, event | category | flops | bytes accessed | tf_op | source)
XLA Modules:
  0.0 591.3 jit_solution(14744341343113099714)
XLA Ops:
  7.3 2.5 pad_maximum_fusion.4
  23.9 4.5 broadcast.237.clone
  29.7 3.1 collective-permute-start
  32.8 23.0 %collective-permute-done = bf16[256,2048]{1,0:T(8,128)(2,1)S(1)} collective-permute-done((bf16[256,2048]{1,0:T(8,128)(2,1)S(1)}, bf16[256,2048]{1,0:T(8,128)(2,1)S(1)}, u32[]{:S(2)}, u32[]{:S(2)}) %collective-permute-start) | collective-permute-done | bytes 1048608 | tf_op jit(solution)/shard_map/ppermute | solution.py:76
  58.1 22.1 %collective-permute-done.2 = bf16[256,2048]{1,0:T(8,128)(2,1)} collective-permute-done((bf16[256,2048]{1,0:T(8,128)(2,1)S(1)}, bf16[256,2048]{1,0:T(8,128)(2,1)}, u32[]{:S(2)}, u32[]{:S(2)}) %collective-permute-start.2) | collective-permute-done | bytes 1048608 | tf_op jit(solution)/shard_map/ppermute | solution.py:76
  83.0 20.9 %collective-permute-done.4 = bf16[256,2048]{1,0:T(8,128)(2,1)S(1)} collective-permute-done((bf16[256,2048]{1,0:T(8,128)(2,1)}, bf16[256,2048]{1,0:T(8,128)(2,1)S(1)}, u32[]{:S(2)}, u32[]{:S(2)}) %collective-permute-start.4) | collective-permute-done | bytes 1048608 | tf_op jit(solution)/shard_map/ppermute | solution.py:76
  113.2 2.3 constant_dynamic-update-slice_fusion.12
  115.5 12.5 %collective-permute-done.10 = bf16[256,2048]{1,0:T(8,128)(2,1)} collective-permute-done((bf16[256,2048]{1,0:T(8,128)(2,1)S(1)}, bf16[256,2048]{1,0:T(8,128)(2,1)}, u32[]{:S(2)}, u32[]{:S(2)}) %collective-permute-start.10) | collective-permute-done | bytes 1048608 | tf_op jit(solution)/shard_map/ppermute | solution.py:76
  130.0 2.3 constant_dynamic-update-slice_fusion.11
  132.4 2.3 constant_dynamic-update-slice_fusion.10
  134.7 2.3 constant_dynamic-update-slice_fusion.9
  139.2 4.4 broadcast.237
  145.8 8.5 %collective-permute-done.11 = bf16[256,2048]{1,0:T(8,128)(2,1)S(1)} collective-permute-done((bf16[256,2048]{1,0:T(8,128)(2,1)}, bf16[256,2048]{1,0:T(8,128)(2,1)S(1)}, u32[]{:S(2)}, u32[]{:S(2)}) %collective-permute-start.11) | collective-permute-done | bytes 1048608 | tf_op jit(solution)/shard_map/ppermute | solution.py:76
  157.4 8.2 %collective-permute-done.6 = bf16[128,2048]{1,0:T(8,128)(2,1)S(1)} collective-permute-done((bf16[128,2048]{1,0:T(8,128)(2,1)S(1)}, bf16[128,2048]{1,0:T(8,128)(2,1)S(1)}, u32[]{:S(2)}, u32[]{:S(2)}) %collective-permute-start.6) | collective-permute-done | bytes 524320 | tf_op jit(solution)/shard_map/ppermute | solution.py:76
  168.1 2.4 constant_dynamic-update-slice_fusion.5
  170.4 2.3 constant_dynamic-update-slice_fusion.4
  173.8 11.3 %collective-permute-done.12 = bf16[256,2048]{1,0:T(8,128)(2,1)S(1)} collective-permute-done((bf16[256,2048]{1,0:T(8,128)(2,1)S(1)}, bf16[256,2048]{1,0:T(8,128)(2,1)S(1)}, u32[]{:S(2)}, u32[]{:S(2)}) %collective-permute-start.12) | collective-permute-done | bytes 1048608 | tf_op jit(solution)/shard_map/ppermute | solution.py:76
  190.8 3.6 collective-permute-done.32
  197.3 18.2 %fusion.300 = (bf16[2048,1280]{0,1:T(8,128)(2,1)}, f32[2048,1280]{0,1:T(8,128)}) fusion(bf16[2048,2048]{1,0:T(8,128)(2,1)} %maximum_dynamic-update-slice_fusion.1, bf16[1280,2048]{1,0:T(8,128)(2,1)} %all-gather.5.cloned.1.call-done), kind=kOutput, calls=%fused_computation.434 | convolution fusion | flops 10740039680 | bytes 29360128 | tf_op jit(solution)/shard_map/gd,fd->gf/dot_general | solution.py:268
  215.5 10.4 %fusion.299 = (bf16[2048,768]{0,1:T(8,128)(2,1)S(1)}, f32[2048,768]{0,1:T(8,128)S(1)}) fusion(f32[768]{0:T(1024)S(1)} %slice-done.7, bf16[2048,2048]{1,0:T(8,128)(2,1)} %maximum_dynamic-update-slice_fusion, bf16[2048,1792]{1,0:T(8,128)(2,1)} %all-gather.3.cloned.1.call-done), kind=kOutput, calls=%fused_computation.433 | convolution fusion | flops 6445596672 | bytes 20974592 | tf_op jit(solution)/shard_map/dot_general | solution.py:209
  249.0 2.3 multiply_reduce_fusion
  260.7 3.0 copy-done.7
  263.7 19.8 %fusion.6 = (bf16[2048,1792]{0,1:T(8,128)(2,1)}, f32[2048,1024]{0,1:T(8,128)}) fusion(bf16[2048,1792]{0,1:T(8,128)(2,1)} %copy-done.7, f32[2048,1280]{0,1:T(8,128)} %get-tuple-element.205, f32[1024]{0:T(1024)S(1)} %slice.525, bf16[2048,2048]{1,0:T(8,128)(2,1)} %maximum_dynamic-update-slice_fusion, bf16[2048,1792]{1,0:T(8,128)(2,1)} %all-gather.3.cloned.1.call-done), kind=kOutput, calls=%fused_computation.14 | convolution fusion | flops 8617197568 | bytes 33558528 | tf_op jit(solution)/shard_map/dot_general | solution.py:216
  283.5 21.1 %convolution_convert_fusion.1 = bf16[2048,1792]{1,0:T(8,128)(2,1)} fusion(bf16[2048,2048]{1,0:T(8,128)(2,1)} %maximum_dynamic-update-slice_fusion, bf16[2048,1792]{0,1:T(8,128)(2,1)} %get-tuple-element.222), kind=kOutput, calls=%fused_computation.12 | convolution fusion | flops 15036055552 | bytes 23068672 | tf_op jit(solution)/shard_map/gd,gf->df/dot_general | solution.py:328
  313.7 6.7 %multiply_convert_fusion = bf16[2048,1024]{0,1:T(8,128)(2,1)S(1)} fusion(f32[2048,1024]{0,1:T(8,128)} %get-tuple-element.223, f32[1024]{0:T(1024)S(1)} %slice.525), kind=kLoop, calls=%fused_computation.9 | loop fusion | flops 12582912 | bytes 12587008 | tf_op jit(solution)/shard_map/convert_element_type | solution.py:220
  321.3 5.0 convolution_convert_fusion.11
  328.1 3.0 convolution_convert_fusion.10
  331.8 3.0 convolution_convert_fusion.9
  336.2 4.1 convolution_convert_fusion.5
  343.3 15.2 %convolution_convert_fusion = bf16[2048,1280]{1,0:T(8,128)(2,1)} fusion(bf16[2048,2048]{1,0:T(8,128)(2,1)} %maximum_dynamic-update-slice_fusion.1, bf16[2048,1024]{0,1:T(8,128)(2,1)S(1)} %multiply_convert_fusion, bf16[2048,256]{0,1:T(8,128)(2,1)S(1)} %copy.39), kind=kOutput, calls=%fused_computation.11 | convolution fusion | flops 10750525440 | bytes 18874368 | tf_op jit(solution)/shard_map/gd,gf->df/dot_general | solution.py:321
  358.6 3.8 fusion.106
  362.4 4.3 convolution_convert_fusion.4
  366.8 3.5 convolution_convert_fusion.3
  377.9 2.2 add_convert_fusion.11
  380.1 9.8 %collective-permute-done.38 = bf16[128,1024]{1,0:T(8,128)(2,1)S(1)} collective-permute-done((bf16[128,1024]{1,0:T(8,128)(2,1)S(1)}, bf16[128,1024]{1,0:T(8,128)(2,1)S(1)}, u32[]{:S(2)}, u32[]{:S(2)}) %collective-permute-start.38) | collective-permute-done | bytes 262176 | tf_op jit(solution)/shard_map/ppermute | solution.py:79
  406.9 23.1 %collective-permute-done.35 = bf16[256,1024]{1,0:T(8,128)(2,1)S(1)} collective-permute-done((bf16[256,1024]{1,0:T(8,128)(2,1)S(1)}, bf16[256,1024]{1,0:T(8,128)(2,1)S(1)}, u32[]{:S(2)}, u32[]{:S(2)}) %collective-permute-start.35) | collective-permute-done | bytes 524320 | tf_op jit(solution)/shard_map/ppermute | solution.py:76
  440.5 6.5 %collective-permute-done.43 = bf16[256,1024]{1,0:T(8,128)(2,1)S(1)} collective-permute-done((bf16[256,1024]{1,0:T(8,128)(2,1)S(1)}, bf16[256,1024]{1,0:T(8,128)(2,1)S(1)}, u32[]{:S(2)}, u32[]{:S(2)}) %collective-permute-start.43) | collective-permute-done | bytes 524320 | tf_op jit(solution)/shard_map/ppermute | solution.py:76
  449.4 6.7 %collective-permute-done.47 = bf16[256,1024]{1,0:T(8,128)(2,1)S(1)} collective-permute-done((bf16[256,1024]{1,0:T(8,128)(2,1)S(1)}, bf16[256,1024]{1,0:T(8,128)(2,1)S(1)}, u32[]{:S(2)}, u32[]{:S(2)}) %collective-permute-start.47) | collective-permute-done | bytes 524320 | tf_op jit(solution)/shard_map/ppermute | solution.py:79
  460.3 17.0 %collective-permute-done.36 = bf16[256,1024]{1,0:T(8,128)(2,1)S(1)} collective-permute-done((bf16[256,1024]{1,0:T(8,128)(2,1)S(1)}, bf16[256,1024]{1,0:T(8,128)(2,1)S(1)}, u32[]{:S(2)}, u32[]{:S(2)}) %collective-permute-start.36) | collective-permute-done | bytes 524320 | tf_op jit(solution)/shard_map/ppermute | solution.py:76
  483.6 7.9 %collective-permute-done.44 = bf16[256,1024]{1,0:T(8,128)(2,1)S(1)} collective-permute-done((bf16[256,1024]{1,0:T(8,128)(2,1)S(1)}, bf16[256,1024]{1,0:T(8,128)(2,1)S(1)}, u32[]{:S(2)}, u32[]{:S(2)}) %collective-permute-start.44) | collective-permute-done | bytes 524320 | tf_op jit(solution)/shard_map/ppermute | solution.py:76
  494.0 5.2 collective-permute-done.48
  507.4 8.1 %collective-permute-done.37 = bf16[256,1024]{1,0:T(8,128)(2,1)S(1)} collective-permute-done((bf16[256,1024]{1,0:T(8,128)(2,1)S(1)}, bf16[256,1024]{1,0:T(8,128)(2,1)S(1)}, u32[]{:S(2)}, u32[]{:S(2)}) %collective-permute-start.37) | collective-permute-done | bytes 524320 | tf_op jit(solution)/shard_map/ppermute | solution.py:76
  517.9 8.8 %collective-permute-done.45 = bf16[256,1024]{1,0:T(8,128)(2,1)S(1)} collective-permute-done((bf16[256,1024]{1,0:T(8,128)(2,1)S(1)}, bf16[256,1024]{1,0:T(8,128)(2,1)S(1)}, u32[]{:S(2)}, u32[]{:S(2)}) %collective-permute-start.45) | collective-permute-done | bytes 524320 | tf_op jit(solution)/shard_map/ppermute | solution.py:76
  528.7 9.9 %collective-permute-done.23 = bf16[256,1024]{1,0:T(8,128)(2,1)S(1)} collective-permute-done((bf16[256,1024]{1,0:T(8,128)(2,1)S(1)}, bf16[256,1024]{1,0:T(8,128)(2,1)S(1)}, u32[]{:S(2)}, u32[]{:S(2)}) %collective-permute-start.23) | collective-permute-done | bytes 524320 | tf_op jit(solution)/shard_map/ppermute | solution.py:79
  539.5 4.7 collective-permute-done.31
  545.1 2.6 convert_reduce_fusion.2
  572.0 2.4 collective-permute-start.56
  579.0 4.2 copy.44
  (387 shorter events, 181.4 us)
Async XLA Ops:
  7.2 190.1 %all-gather.5.cloned.1.call-start = ((), (), s32[]{:S(2)}) async-start(), calls=%async_computation.3 | async-start | bytes 6553600 | tf_op jit(solution)/shard_map/all_gather | solution.py:192
  9.8 205.7 %all-gather.3.cloned.1.call-start = ((), (), s32[]{:S(2)}) async-start(), calls=%async_computation.2 | async-start | bytes 9175040 | tf_op jit(solution)/shard_map/all_gather | solution.py:185
  13.9 539.2 %reduce-scatter.3.cloned.1.call-start = ((), (), s32[]{:S(2)}) async-start(), calls=%async_computation.4 | async-start | bytes 9175040 | tf_op jit(solution)/shard_map/reduce_scatter | solution.py:327
  29.7 26.1 %collective-permute-start = (bf16[256,2048]{1,0:T(8,128)(2,1)S(1)}, bf16[256,2048]{1,0:T(8,128)(2,1)S(1)}, u32[]{:S(2)}, u32[]{:S(2)}) collective-permute-start(bf16[256,2048]{1,0:T(8,128)(2,1)S(1)} %get-tuple-element.169), channel_id=1, source_target_pairs={{0,2},{2,4},{4,6},{6,7},{7,5},{5,3},{3,1},{1,0},{8,10},{10,12},{12... | collective-permute-start | bytes 3145736 | tf_op jit(solution)/shard_map/ppermute | solution.py:76
  32.8 24.9 %collective-permute-start.1 = (bf16[256,2048]{1,0:T(8,128)(2,1)S(1)}, bf16[256,2048]{1,0:T(8,128)(2,1)S(1)}, u32[]{:S(2)}, u32[]{:S(2)}) collective-permute-start(bf16[256,2048]{1,0:T(8,128)(2,1)S(1)} %get-tuple-element.169), channel_id=1, source_target_pairs={{0,1},{2,0},{4,2},{6,4},{7,6},{5,7},{3,5},{1,3},{8,9},{10,8},{12,1... | collective-permute-start | bytes 3145736 | tf_op jit(solution)/shard_map/ppermute | solution.py:79
  55.8 24.4 %collective-permute-start.2 = (bf16[256,2048]{1,0:T(8,128)(2,1)S(1)}, bf16[256,2048]{1,0:T(8,128)(2,1)}, u32[]{:S(2)}, u32[]{:S(2)}) collective-permute-start(bf16[256,2048]{1,0:T(8,128)(2,1)S(1)} %collective-permute-done), channel_id=1, source_target_pairs={{0,2},{2,4},{4,6},{6,7},{7,5},{5,3},{3,1},{1,0},{8,10},{10,12},{12... | collective-permute-start | bytes 3145736 | tf_op jit(solution)/shard_map/ppermute | solution.py:76
  57.7 24.1 %collective-permute-start.3 = (bf16[256,2048]{1,0:T(8,128)(2,1)S(1)}, bf16[256,2048]{1,0:T(8,128)(2,1)}, u32[]{:S(2)}, u32[]{:S(2)}) collective-permute-start(bf16[256,2048]{1,0:T(8,128)(2,1)S(1)} %collective-permute-done.1), channel_id=1, source_target_pairs={{0,1},{2,0},{4,2},{6,4},{7,6},{5,7},{3,5},{1,3},{8,9},{10,8},{12,1... | collective-permute-start | bytes 3145736 | tf_op jit(solution)/shard_map/ppermute | solution.py:79
  57.8 49.0 %collective-permute-start.8 = (f32[1,1792]{1,0:T(1,128)S(1)}, f32[1,1792]{1,0:T(1,128)S(1)}, u32[]{:S(2)}, u32[]{:S(2)}) collective-permute-start(f32[1,1792]{1,0:T(1,128)S(1)} %broadcast_in_dim.26), channel_id=1, source_target_pairs={{0,8},{8,0},{16,24},{24,16},{1,9},{9,1},{17,25},{25,17},{2,10},{10... | collective-permute-start | bytes 21512 | tf_op jit(solution)/shard_map/ppermute | solution.py:125
  80.2 23.6 %collective-permute-start.4 = (bf16[256,2048]{1,0:T(8,128)(2,1)}, bf16[256,2048]{1,0:T(8,128)(2,1)S(1)}, u32[]{:S(2)}, u32[]{:S(2)}) collective-permute-start(bf16[256,2048]{1,0:T(8,128)(2,1)} %collective-permute-done.2), channel_id=1, source_target_pairs={{0,2},{2,4},{4,6},{6,7},{7,5},{5,3},{3,1},{1,0},{8,10},{10,12},{12... | collective-permute-start | bytes 3145736 | tf_op jit(solution)/shard_map/ppermute | solution.py:76
  81.8 23.1 %collective-permute-start.5 = (bf16[256,2048]{1,0:T(8,128)(2,1)}, bf16[256,2048]{1,0:T(8,128)(2,1)S(1)}, u32[]{:S(2)}, u32[]{:S(2)}) collective-permute-start(bf16[256,2048]{1,0:T(8,128)(2,1)} %collective-permute-done.3), channel_id=1, source_target_pairs={{0,1},{2,0},{4,2},{6,4},{7,6},{5,7},{3,5},{1,3},{8,9},{10,8},{12,1... | collective-permute-start | bytes 3145736 | tf_op jit(solution)/shard_map/ppermute | solution.py:79
  104.9 23.1 %collective-permute-start.10 = (bf16[256,2048]{1,0:T(8,128)(2,1)S(1)}, bf16[256,2048]{1,0:T(8,128)(2,1)}, u32[]{:S(2)}, u32[]{:S(2)}) collective-permute-start(bf16[256,2048]{1,0:T(8,128)(2,1)S(1)} %copy-done.11), channel_id=1, source_target_pairs={{0,2},{2,4},{4,6},{6,7},{7,5},{5,3},{3,1},{1,0},{8,10},{10,12},{12... | collective-permute-start | bytes 3145736 | tf_op jit(solution)/shard_map/ppermute | solution.py:76
  106.4 23.1 %collective-permute-start.13 = (bf16[256,2048]{1,0:T(8,128)(2,1)S(1)}, bf16[256,2048]{1,0:T(8,128)(2,1)}, u32[]{:S(2)}, u32[]{:S(2)}) collective-permute-start(bf16[256,2048]{1,0:T(8,128)(2,1)S(1)} %copy-done.11), channel_id=1, source_target_pairs={{0,1},{2,0},{4,2},{6,4},{7,6},{5,7},{3,5},{1,3},{8,9},{10,8},{12,1... | collective-permute-start | bytes 3145736 | tf_op jit(solution)/shard_map/ppermute | solution.py:79
  128.0 26.3 %collective-permute-start.11 = (bf16[256,2048]{1,0:T(8,128)(2,1)}, bf16[256,2048]{1,0:T(8,128)(2,1)S(1)}, u32[]{:S(2)}, u32[]{:S(2)}) collective-permute-start(bf16[256,2048]{1,0:T(8,128)(2,1)} %collective-permute-done.10), channel_id=1, source_target_pairs={{0,2},{2,4},{4,6},{6,7},{7,5},{5,3},{3,1},{1,0},{8,10},{10,12},{12... | collective-permute-start | bytes 3145736 | tf_op jit(solution)/shard_map/ppermute | solution.py:76
  129.5 26.3 %collective-permute-start.14 = (bf16[256,2048]{1,0:T(8,128)(2,1)}, bf16[256,2048]{1,0:T(8,128)(2,1)S(1)}, u32[]{:S(2)}, u32[]{:S(2)}) collective-permute-start(bf16[256,2048]{1,0:T(8,128)(2,1)} %collective-permute-done.13), channel_id=1, source_target_pairs={{0,1},{2,0},{4,2},{6,4},{7,6},{5,7},{3,5},{1,3},{8,9},{10,8},{12,1... | collective-permute-start | bytes 3145736 | tf_op jit(solution)/shard_map/ppermute | solution.py:79
  137.0 28.5 %collective-permute-start.6 = (bf16[128,2048]{1,0:T(8,128)(2,1)S(1)}, bf16[128,2048]{1,0:T(8,128)(2,1)S(1)}, u32[]{:S(2)}, u32[]{:S(2)}) collective-permute-start(bf16[128,2048]{1,0:T(8,128)(2,1)S(1)} %slice.502), channel_id=1, source_target_pairs={{0,2},{2,4},{4,6},{6,7},{7,5},{5,3},{3,1},{1,0},{8,10},{10,12},{12... | collective-permute-start | bytes 1572872 | tf_op jit(solution)/shard_map/ppermute | solution.py:76
  138.6 28.5 %collective-permute-start.7 = (bf16[128,2048]{1,0:T(8,128)(2,1)S(1)}, bf16[128,2048]{1,0:T(8,128)(2,1)S(1)}, u32[]{:S(2)}, u32[]{:S(2)}) collective-permute-start(bf16[128,2048]{1,0:T(8,128)(2,1)S(1)} %slice.503), channel_id=1, source_target_pairs={{0,1},{2,0},{4,2},{6,4},{7,6},{5,7},{3,5},{1,3},{8,9},{10,8},{12,1... | collective-permute-start | bytes 1572872 | tf_op jit(solution)/shard_map/ppermute | solution.py:79
  154.3 30.8 %collective-permute-start.12 = (bf16[256,2048]{1,0:T(8,128)(2,1)S(1)}, bf16[256,2048]{1,0:T(8,128)(2,1)S(1)}, u32[]{:S(2)}, u32[]{:S(2)}) collective-permute-start(bf16[256,2048]{1,0:T(8,128)(2,1)S(1)} %collective-permute-done.11), channel_id=1, source_target_pairs={{0,2},{2,4},{4,6},{6,7},{7,5},{5,3},{3,1},{1,0},{8,10},{10,12},{12... | collective-permute-start | bytes 3145736 | tf_op jit(solution)/shard_map/ppermute | solution.py:76
  155.8 30.9 %collective-permute-start.15 = (bf16[256,2048]{1,0:T(8,128)(2,1)S(1)}, bf16[256,2048]{1,0:T(8,128)(2,1)S(1)}, u32[]{:S(2)}, u32[]{:S(2)}) collective-permute-start(bf16[256,2048]{1,0:T(8,128)(2,1)S(1)} %collective-permute-done.14), channel_id=1, source_target_pairs={{0,1},{2,0},{4,2},{6,4},{7,6},{5,7},{3,5},{1,3},{8,9},{10,8},{12,1... | collective-permute-start | bytes 3145736 | tf_op jit(solution)/shard_map/ppermute | solution.py:79
  304.6 269.8 %reduce-scatter.5.cloned.1.call-start = ((), (), s32[]{:S(2)}) async-start(), calls=%async_computation.5 | async-start | bytes 6553600 | tf_op jit(solution)/shard_map/reduce_scatter | solution.py:320
  326.2 66.3 %collective-permute-start.16 = (bf16[128,1024]{1,0:T(8,128)(2,1)}, bf16[128,1024]{1,0:T(8,128)(2,1)}, u32[]{:S(2)}, u32[]{:S(2)}) collective-permute-start(bf16[128,1024]{1,0:T(8,128)(2,1)} %convolution_convert_fusion.11), channel_id=1, source_target_pairs={{0,2},{2,4},{4,6},{6,7},{7,5},{5,3},{3,1},{1,0},{8,10},{10,12},{12... | collective-permute-start | bytes 786440 | tf_op jit(solution)/shard_map/ppermute | solution.py:76
  331.1 63.9 %collective-permute-start.20 = (bf16[128,1024]{1,0:T(8,128)(2,1)}, bf16[128,1024]{1,0:T(8,128)(2,1)}, u32[]{:S(2)}, u32[]{:S(2)}) collective-permute-start(bf16[128,1024]{1,0:T(8,128)(2,1)} %convolution_convert_fusion.10), channel_id=1, source_target_pairs={{0,1},{2,0},{4,2},{6,4},{7,6},{5,7},{3,5},{1,3},{8,9},{10,8},{12,1... | collective-permute-start | bytes 786440 | tf_op jit(solution)/shard_map/ppermute | solution.py:79
  334.8 63.6 %collective-permute-start.24 = (bf16[128,1024]{1,0:T(8,128)(2,1)}, bf16[128,1024]{1,0:T(8,128)(2,1)S(1)}, u32[]{:S(2)}, u32[]{:S(2)}) collective-permute-start(bf16[128,1024]{1,0:T(8,128)(2,1)} %convolution_convert_fusion.9), channel_id=1, source_target_pairs={{0,2},{2,4},{4,6},{6,7},{7,5},{5,3},{3,1},{1,0},{8,10},{10,12},{12... | collective-permute-start | bytes 786440 | tf_op jit(solution)/shard_map/ppermute | solution.py:76
  340.3 36.9 %collective-permute-start.34 = (bf16[128,1024]{1,0:T(8,128)(2,1)}, bf16[128,1024]{1,0:T(8,128)(2,1)}, u32[]{:S(2)}, u32[]{:S(2)}) collective-permute-start(bf16[128,1024]{1,0:T(8,128)(2,1)} %convolution_convert_fusion.5), channel_id=1, source_target_pairs={{0,2},{2,4},{4,6},{6,7},{7,5},{5,3},{3,1},{1,0},{8,10},{10,12},{12... | collective-permute-start | bytes 786440 | tf_op jit(solution)/shard_map/ppermute | solution.py:76
  343.3 29.7 %collective-permute-start.50 = (f32[1,1792]{1,0:T(1,128)S(1)}, f32[1,1792]{1,0:T(1,128)S(1)}, u32[]{:S(2)}, u32[]{:S(2)}) collective-permute-start(f32[1,1792]{1,0:T(1,128)S(1)} %broadcast_in_dim.32), channel_id=1, source_target_pairs={{0,8},{8,0},{16,24},{24,16},{1,9},{9,1},{17,25},{25,17},{2,10},{10... | collective-permute-start | bytes 21512 | tf_op jit(solution)/shard_map/ppermute | solution.py:125
  376.7 28.0 %collective-permute-start.28 = (bf16[128,1024]{1,0:T(8,128)(2,1)S(1)}, bf16[128,1024]{1,0:T(8,128)(2,1)S(1)}, u32[]{:S(2)}, u32[]{:S(2)}) collective-permute-start(bf16[128,1024]{1,0:T(8,128)(2,1)S(1)} %convolution_convert_fusion.8), channel_id=1, source_target_pairs={{0,1},{2,0},{4,2},{6,4},{7,6},{5,7},{3,5},{1,3},{8,9},{10,8},{12,1... | collective-permute-start | bytes 786440 | tf_op jit(solution)/shard_map/ppermute | solution.py:79
  395.0 39.6 %collective-permute-start.17 = (bf16[256,1024]{1,0:T(8,128)(2,1)S(1)}, bf16[256,1024]{1,0:T(8,128)(2,1)S(1)}, u32[]{:S(2)}, u32[]{:S(2)}) collective-permute-start(bf16[256,1024]{1,0:T(8,128)(2,1)S(1)} %fusion.62), channel_id=1, source_target_pairs={{0,2},{2,4},{4,6},{6,7},{7,5},{5,3},{3,1},{1,0},{8,10},{10,12},{12... | collective-permute-start | bytes 1572872 | tf_op jit(solution)/shard_map/ppermute | solution.py:76
  398.4 37.9 %collective-permute-start.21 = (bf16[256,1024]{1,0:T(8,128)(2,1)S(1)}, bf16[256,1024]{1,0:T(8,128)(2,1)S(1)}, u32[]{:S(2)}, u32[]{:S(2)}) collective-permute-start(bf16[256,1024]{1,0:T(8,128)(2,1)S(1)} %fusion.65), channel_id=1, source_target_pairs={{0,1},{2,0},{4,2},{6,4},{7,6},{5,7},{3,5},{1,3},{8,9},{10,8},{12,1... | collective-permute-start | bytes 1572872 | tf_op jit(solution)/shard_map/ppermute | solution.py:79
  399.9 38.6 %collective-permute-start.25 = (bf16[256,1024]{1,0:T(8,128)(2,1)S(1)}, bf16[256,1024]{1,0:T(8,128)(2,1)S(1)}, u32[]{:S(2)}, u32[]{:S(2)}) collective-permute-start(bf16[256,1024]{1,0:T(8,128)(2,1)S(1)} %fusion.68), channel_id=1, source_target_pairs={{0,2},{2,4},{4,6},{6,7},{7,5},{5,3},{3,1},{1,0},{8,10},{10,12},{12... | collective-permute-start | bytes 1572872 | tf_op jit(solution)/shard_map/ppermute | solution.py:76
  402.7 27.4 %collective-permute-start.35 = (bf16[256,1024]{1,0:T(8,128)(2,1)S(1)}, bf16[256,1024]{1,0:T(8,128)(2,1)S(1)}, u32[]{:S(2)}, u32[]{:S(2)}) collective-permute-start(bf16[256,1024]{1,0:T(8,128)(2,1)S(1)} %add_convert_fusion.11), channel_id=1, source_target_pairs={{0,2},{2,4},{4,6},{6,7},{7,5},{5,3},{3,1},{1,0},{8,10},{10,12},{12... | collective-permute-start | bytes 1572872 | tf_op jit(solution)/shard_map/ppermute | solution.py:76
  404.7 27.4 %collective-permute-start.39 = (bf16[256,1024]{1,0:T(8,128)(2,1)S(1)}, bf16[256,1024]{1,0:T(8,128)(2,1)S(1)}, u32[]{:S(2)}, u32[]{:S(2)}) collective-permute-start(bf16[256,1024]{1,0:T(8,128)(2,1)S(1)} %add_convert_fusion.8), channel_id=1, source_target_pairs={{0,1},{2,0},{4,2},{6,4},{7,6},{5,7},{3,5},{1,3},{8,9},{10,8},{12,1... | collective-permute-start | bytes 1572872 | tf_op jit(solution)/shard_map/ppermute | solution.py:79
  430.1 28.8 %collective-permute-start.29 = (bf16[256,1024]{1,0:T(8,128)(2,1)S(1)}, bf16[256,1024]{1,0:T(8,128)(2,1)S(1)}, u32[]{:S(2)}, u32[]{:S(2)}) collective-permute-start(bf16[256,1024]{1,0:T(8,128)(2,1)S(1)} %fusion.71), channel_id=1, source_target_pairs={{0,1},{2,0},{4,2},{6,4},{7,6},{5,7},{3,5},{1,3},{8,9},{10,8},{12,1... | collective-permute-start | bytes 1572872 | tf_op jit(solution)/shard_map/ppermute | solution.py:79
  432.1 14.9 %collective-permute-start.43 = (bf16[256,1024]{1,0:T(8,128)(2,1)S(1)}, bf16[256,1024]{1,0:T(8,128)(2,1)S(1)}, u32[]{:S(2)}, u32[]{:S(2)}) collective-permute-start(bf16[256,1024]{1,0:T(8,128)(2,1)S(1)} %add_convert_fusion.5), channel_id=1, source_target_pairs={{0,2},{2,4},{4,6},{6,7},{7,5},{5,3},{3,1},{1,0},{8,10},{10,12},{12... | collective-permute-start | bytes 1572872 | tf_op jit(solution)/shard_map/ppermute | solution.py:76
  434.6 21.6 %collective-permute-start.47 = (bf16[256,1024]{1,0:T(8,128)(2,1)S(1)}, bf16[256,1024]{1,0:T(8,128)(2,1)S(1)}, u32[]{:S(2)}, u32[]{:S(2)}) collective-permute-start(bf16[256,1024]{1,0:T(8,128)(2,1)S(1)} %add_convert_fusion.2), channel_id=1, source_target_pairs={{0,1},{2,0},{4,2},{6,4},{7,6},{5,7},{3,5},{1,3},{8,9},{10,8},{12,1... | collective-permute-start | bytes 1572872 | tf_op jit(solution)/shard_map/ppermute | solution.py:79
  436.3 45.5 %collective-permute-start.18 = (bf16[256,1024]{1,0:T(8,128)(2,1)S(1)}, bf16[256,1024]{1,0:T(8,128)(2,1)S(1)}, u32[]{:S(2)}, u32[]{:S(2)}) collective-permute-start(bf16[256,1024]{1,0:T(8,128)(2,1)S(1)} %fusion.61), channel_id=1, source_target_pairs={{0,2},{2,4},{4,6},{6,7},{7,5},{5,3},{3,1},{1,0},{8,10},{10,12},{12... | collective-permute-start | bytes 1572872 | tf_op jit(solution)/shard_map/ppermute | solution.py:76
  438.5 62.7 %collective-permute-start.22 = (bf16[256,1024]{1,0:T(8,128)(2,1)S(1)}, bf16[256,1024]{1,0:T(8,128)(2,1)S(1)}, u32[]{:S(2)}, u32[]{:S(2)}) collective-permute-start(bf16[256,1024]{1,0:T(8,128)(2,1)S(1)} %fusion.64), channel_id=1, source_target_pairs={{0,1},{2,0},{4,2},{6,4},{7,6},{5,7},{3,5},{1,3},{8,9},{10,8},{12,1... | collective-permute-start | bytes 1572872 | tf_op jit(solution)/shard_map/ppermute | solution.py:79
  447.0 56.4 %collective-permute-start.26 = (bf16[256,1024]{1,0:T(8,128)(2,1)S(1)}, bf16[256,1024]{1,0:T(8,128)(2,1)S(1)}, u32[]{:S(2)}, u32[]{:S(2)}) collective-permute-start(bf16[256,1024]{1,0:T(8,128)(2,1)S(1)} %fusion.67), channel_id=1, source_target_pairs={{0,2},{2,4},{4,6},{6,7},{7,5},{5,3},{3,1},{1,0},{8,10},{10,12},{12... | collective-permute-start | bytes 1572872 | tf_op jit(solution)/shard_map/ppermute | solution.py:76
  456.2 21.2 %collective-permute-start.36 = (bf16[256,1024]{1,0:T(8,128)(2,1)S(1)}, bf16[256,1024]{1,0:T(8,128)(2,1)S(1)}, u32[]{:S(2)}, u32[]{:S(2)}) collective-permute-start(bf16[256,1024]{1,0:T(8,128)(2,1)S(1)} %add_convert_fusion.10), channel_id=1, source_target_pairs={{0,2},{2,4},{4,6},{6,7},{7,5},{5,3},{3,1},{1,0},{8,10},{10,12},{12... | collective-permute-start | bytes 1572872 | tf_op jit(solution)/shard_map/ppermute | solution.py:76
  458.9 20.4 %collective-permute-start.40 = (bf16[256,1024]{1,0:T(8,128)(2,1)S(1)}, bf16[256,1024]{1,0:T(8,128)(2,1)S(1)}, u32[]{:S(2)}, u32[]{:S(2)}) collective-permute-start(bf16[256,1024]{1,0:T(8,128)(2,1)S(1)} %add_convert_fusion.7), channel_id=1, source_target_pairs={{0,1},{2,0},{4,2},{6,4},{7,6},{5,7},{3,5},{1,3},{8,9},{10,8},{12,1... | collective-permute-start | bytes 1572872 | tf_op jit(solution)/shard_map/ppermute | solution.py:79
  477.4 27.8 %collective-permute-start.30 = (bf16[256,1024]{1,0:T(8,128)(2,1)S(1)}, bf16[256,1024]{1,0:T(8,128)(2,1)S(1)}, u32[]{:S(2)}, u32[]{:S(2)}) collective-permute-start(bf16[256,1024]{1,0:T(8,128)(2,1)S(1)} %fusion.70), channel_id=1, source_target_pairs={{0,1},{2,0},{4,2},{6,4},{7,6},{5,7},{3,5},{1,3},{8,9},{10,8},{12,1... | collective-permute-start | bytes 1572872 | tf_op jit(solution)/shard_map/ppermute | solution.py:79
  481.9 17.3 %collective-permute-start.48 = (bf16[256,1024]{1,0:T(8,128)(2,1)S(1)}, bf16[256,1024]{1,0:T(8,128)(2,1)S(1)}, u32[]{:S(2)}, u32[]{:S(2)}) collective-permute-start(bf16[256,1024]{1,0:T(8,128)(2,1)S(1)} %add_convert_fusion.1), channel_id=1, source_target_pairs={{0,1},{2,0},{4,2},{6,4},{7,6},{5,7},{3,5},{1,3},{8,9},{10,8},{12,1... | collective-permute-start | bytes 1572872 | tf_op jit(solution)/shard_map/ppermute | solution.py:79
  491.5 37.2 %collective-permute-start.19 = (bf16[256,1024]{1,0:T(8,128)(2,1)S(1)}, bf16[256,1024]{1,0:T(8,128)(2,1)S(1)}, u32[]{:S(2)}, u32[]{:S(2)}) collective-permute-start(bf16[256,1024]{1,0:T(8,128)(2,1)S(1)} %fusion.60), channel_id=1, source_target_pairs={{0,2},{2,4},{4,6},{6,7},{7,5},{5,3},{3,1},{1,0},{8,10},{10,12},{12... | collective-permute-start | bytes 1572872 | tf_op jit(solution)/shard_map/ppermute | solution.py:76
  499.2 16.3 %collective-permute-start.37 = (bf16[256,1024]{1,0:T(8,128)(2,1)S(1)}, bf16[256,1024]{1,0:T(8,128)(2,1)S(1)}, u32[]{:S(2)}, u32[]{:S(2)}) collective-permute-start(bf16[256,1024]{1,0:T(8,128)(2,1)S(1)} %add_convert_fusion.9), channel_id=1, source_target_pairs={{0,2},{2,4},{4,6},{6,7},{7,5},{5,3},{3,1},{1,0},{8,10},{10,12},{12... | collective-permute-start | bytes 1572872 | tf_op jit(solution)/shard_map/ppermute | solution.py:76
  501.2 15.1 %collective-permute-start.41 = (bf16[256,1024]{1,0:T(8,128)(2,1)S(1)}, bf16[256,1024]{1,0:T(8,128)(2,1)S(1)}, u32[]{:S(2)}, u32[]{:S(2)}) collective-permute-start(bf16[256,1024]{1,0:T(8,128)(2,1)S(1)} %add_convert_fusion.6), channel_id=1, source_target_pairs={{0,1},{2,0},{4,2},{6,4},{7,6},{5,7},{3,5},{1,3},{8,9},{10,8},{12,1... | collective-permute-start | bytes 1572872 | tf_op jit(solution)/shard_map/ppermute | solution.py:79
  503.4 23.3 %collective-permute-start.45 = (bf16[256,1024]{1,0:T(8,128)(2,1)S(1)}, bf16[256,1024]{1,0:T(8,128)(2,1)S(1)}, u32[]{:S(2)}, u32[]{:S(2)}) collective-permute-start(bf16[256,1024]{1,0:T(8,128)(2,1)S(1)} %add_convert_fusion.3), channel_id=1, source_target_pairs={{0,2},{2,4},{4,6},{6,7},{7,5},{5,3},{3,1},{1,0},{8,10},{10,12},{12... | collective-permute-start | bytes 1572872 | tf_op jit(solution)/shard_map/ppermute | solution.py:76
  505.2 22.7 %collective-permute-start.49 = (bf16[256,1024]{1,0:T(8,128)(2,1)S(1)}, bf16[256,1024]{1,0:T(8,128)(2,1)S(1)}, u32[]{:S(2)}, u32[]{:S(2)}) collective-permute-start(bf16[256,1024]{1,0:T(8,128)(2,1)S(1)} %add_convert_fusion), channel_id=1, source_target_pairs={{0,1},{2,0},{4,2},{6,4},{7,6},{5,7},{3,5},{1,3},{8,9},{10,8},{12,1... | collective-permute-start | bytes 1572872 | tf_op jit(solution)/shard_map/ppermute | solution.py:79
  515.5 23.1 %collective-permute-start.23 = (bf16[256,1024]{1,0:T(8,128)(2,1)S(1)}, bf16[256,1024]{1,0:T(8,128)(2,1)S(1)}, u32[]{:S(2)}, u32[]{:S(2)}) collective-permute-start(bf16[256,1024]{1,0:T(8,128)(2,1)S(1)} %fusion.63), channel_id=1, source_target_pairs={{0,1},{2,0},{4,2},{6,4},{7,6},{5,7},{3,5},{1,3},{8,9},{10,8},{12,1... | collective-permute-start | bytes 1572872 | tf_op jit(solution)/shard_map/ppermute | solution.py:79
  516.4 23.1 %collective-permute-start.27 = (bf16[256,1024]{1,0:T(8,128)(2,1)S(1)}, bf16[256,1024]{1,0:T(8,128)(2,1)S(1)}, u32[]{:S(2)}, u32[]{:S(2)}) collective-permute-start(bf16[256,1024]{1,0:T(8,128)(2,1)S(1)} %fusion.66), channel_id=1, source_target_pairs={{0,2},{2,4},{4,6},{6,7},{7,5},{5,3},{3,1},{1,0},{8,10},{10,12},{12... | collective-permute-start | bytes 1572872 | tf_op jit(solution)/shard_map/ppermute | solution.py:76
  526.7 17.4 %collective-permute-start.31 = (bf16[256,1024]{1,0:T(8,128)(2,1)S(1)}, bf16[256,1024]{1,0:T(8,128)(2,1)S(1)}, u32[]{:S(2)}, u32[]{:S(2)}) collective-permute-start(bf16[256,1024]{1,0:T(8,128)(2,1)S(1)} %fusion.69), channel_id=1, source_target_pairs={{0,1},{2,0},{4,2},{6,4},{7,6},{5,7},{3,5},{1,3},{8,9},{10,8},{12,1... | collective-permute-start | bytes 1572872 | tf_op jit(solution)/shard_map/ppermute | solution.py:79
  (71 other events, 849.6 us)
Sparse Core Ops, SparseCore 0:
  10.2 43.1 all-gather.4
  55.5 52.4 all-gather.2
  304.7 64.9 reduce-scatter.2
  372.3 51.3 reduce-scatter.4
